TPU v7x, 32 devices: a whole 2x2x4 slice. The times are simulated.
32 devices in a mesh: fsdp: 2 (over x), ctx: 4 (over y, core), tp: 4 (over z).
Axes of the slice: x: 2, y: 2, z: 4, core: 2. Of those that a mesh axis runs over, the one named last changes fastest.
Arguments:
- inputs: bfloat16 [4, 16, 196, 768], P('fsdp', 'ctx', 'tp'), may hold values from -6 to 6
- cotangent: bfloat16 [4, 16, 196, 768], P('fsdp', 'ctx', 'tp'), may hold values from -6 to 6
- norm_gain: float32 [3, 768], replicated, may hold values from 0.5 to 1.5
- norm_bias: float32 [3, 768], replicated, may hold values from -1 to 1
- attn_weight: bfloat16 [2, 3, 768, 768], P(None, None, 'fsdp', 'tp'), may hold values from -0.21875 to 0.21875
- attn_bias: float32 [2, 2, 768], P(None, None, 'tp'), may hold values from -1 to 1
- out_weight: bfloat16 [2, 768, 768], P(None, 'tp', 'fsdp'), may hold values from -0.625 to 0.625
- out_bias: float32 [2, 768], replicated, may hold values from -1 to 1
- up_weight: bfloat16 [768, 3072], P('fsdp', 'tp'), may hold values from -0.21875 to 0.21875
- up_bias: float32 [3072], replicated, may hold values from -1 to 1
- down_weight: bfloat16 [3072, 768], P('tp', 'fsdp'), may hold values from -0.109375 to 0.109375
- down_bias: float32 [768], replicated, may hold values from -1 to 1
Outputs:
- outputs: bfloat16 [4, 16, 196, 768], P('fsdp', 'ctx', 'tp')
- input_grad: bfloat16 [4, 16, 196, 768], P('fsdp', 'ctx', 'tp')
- grad_norm_gain: float32 [3, 768], replicated
- grad_norm_bias: float32 [3, 768], replicated
- grad_attn_weight: float32 [2, 3, 768, 768], P(None, None, ('fsdp', 'ctx'), 'tp')
- grad_attn_bias: float32 [2, 2, 768], P(None, None, 'tp')
- grad_out_weight: float32 [2, 768, 768], P(None, 'tp', ('fsdp', 'ctx'))
- grad_out_bias: float32 [2, 768], replicated
- grad_up_weight: float32 [768, 3072], P(('fsdp', 'ctx'), 'tp')
- grad_up_bias: float32 [3072], replicated
- grad_down_weight: float32 [3072, 768], P('tp', ('fsdp', 'ctx'))
- grad_down_bias: float32 [768], replicated
All inputs are finite; a program needn't handle non-finite values.
Results may differ from a plain program's by a relative error of at most 0.025.
Values may be sent and summed in bfloat16 or wider, within the bound.
A program may use at most 128 MiB of HBM per device.

v0:
```python
import jax
import jax.numpy as jnp
from jax import lax
from jax.sharding import PartitionSpec as P

HEAD = 64
EPSILON = 1e-06


def layer_norm(rows, gain, shift):
    centre = rows - jnp.mean(rows, axis=-1, keepdims=True)
    spread = jnp.mean(centre * centre, axis=-1, keepdims=True)
    return centre * lax.rsqrt(spread + EPSILON) * gain + shift


def gelu_exact(values):
    return jax.nn.gelu(values, approximate=False)


def split_heads(values):
    return values.reshape(values.shape[:-1] + (values.shape[-1] // HEAD, HEAD))


def einsum_forms(temporal):
    if temporal:
        return ("qbhe,kbhe->bhqk", "bhqk,kbhe->qbhe", "bhqk,qbhe->kbhe")
    return ("bqhe,bkhe->bhqk", "bhqk,bkhe->bqhe", "bhqk,bqhe->bkhe")


def scores_of(queries, key_rows, temporal):
    score_form = einsum_forms(temporal)[0]
    return jnp.einsum(score_form, queries, key_rows, preferred_element_type=jnp.float32) * 0.125


def attend(triple, temporal):
    mix_form = einsum_forms(temporal)[1]
    queries, key_rows, value_rows = (
        split_heads(triple[0]),
        split_heads(triple[1]),
        split_heads(triple[2]),
    )
    scores = scores_of(queries, key_rows, temporal)
    highest = jnp.max(scores, axis=-1, keepdims=True)
    log_total = highest + jnp.log(jnp.sum(jnp.exp(scores - highest), axis=-1, keepdims=True))
    weights = jnp.exp(scores - log_total).astype(jnp.bfloat16)
    mixed = jnp.einsum(mix_form, weights, value_rows, preferred_element_type=jnp.float32)
    return (mixed.reshape(triple.shape[1:]).astype(jnp.bfloat16), log_total)


def attend_back(triple, log_total, grad_mixed, temporal):
    score_form, mix_form, back_form = einsum_forms(temporal)
    queries, key_rows, value_rows = (
        split_heads(triple[0]),
        split_heads(triple[1]),
        split_heads(triple[2]),
    )
    probs = jnp.exp(scores_of(queries, key_rows, temporal) - log_total)
    weights = probs.astype(jnp.bfloat16)
    grad_heads = split_heads(grad_mixed)
    grad_probs = jnp.einsum(score_form, grad_heads, value_rows, preferred_element_type=jnp.float32)
    inner = jnp.sum(probs * grad_probs, axis=-1, keepdims=True)
    grad_scores = (probs * (grad_probs - inner)).astype(jnp.bfloat16)
    grad_query = (
        jnp.einsum(mix_form, grad_scores, key_rows, preferred_element_type=jnp.float32) * 0.125
    )
    grad_key = (
        jnp.einsum(back_form, grad_scores, queries, preferred_element_type=jnp.float32) * 0.125
    )
    grad_value = jnp.einsum(back_form, weights, grad_heads, preferred_element_type=jnp.float32)
    stacked = jnp.stack([grad_query, grad_key, grad_value]).astype(jnp.bfloat16)
    return stacked.reshape(triple.shape)


def local(
    inputs,
    cotangent,
    norm_gain,
    norm_bias,
    attn_weight,
    attn_bias,
    out_weight,
    out_bias,
    up_weight,
    up_bias,
    down_weight,
    down_bias,
):
    width = attn_weight.shape[3]
    hidden_width = up_weight.shape[1]
    model_width = inputs.shape[3]
    tp_rank = lax.axis_index("tp")
    up_wide, down_wide = (up_weight, down_weight)
    up_bias_used = lax.dynamic_slice_in_dim(up_bias, tp_rank * hidden_width, hidden_width, 0)
    used_hidden = up_wide.shape[1]

    def fetch_weights():
        return (
            lax.all_gather(attn_weight, "fsdp", axis=2, tiled=True),
            lax.all_gather(out_weight, "fsdp", axis=2, tiled=True),
            lax.all_gather(up_wide, "fsdp", axis=0, tiled=True),
            lax.all_gather(down_wide, "fsdp", axis=1, tiled=True),
        )

    def spread_rows(values):
        return lax.all_gather(values, "tp", axis=1, tiled=True)

    def sum_rows(values):
        return lax.psum_scatter(
            values.astype(jnp.bfloat16), "tp", scatter_dimension=1, tiled=True
        ).astype(jnp.float32)

    def spread_grads(values):
        return lax.all_gather(values, "tp", axis=1, tiled=True)

    def sum_grads(values):
        return lax.psum_scatter(
            values.astype(jnp.bfloat16), "tp", scatter_dimension=1, tiled=True
        ).astype(jnp.float32)

    def attn_forward(stream, index, weights_all, temporal):
        attn_full, out_full = (weights_all[0], weights_all[1])
        normed = spread_rows(
            layer_norm(stream, norm_gain[index], norm_bias[index]).astype(jnp.bfloat16)
        )
        zero_row = jnp.zeros((width,), jnp.float32)
        bias_rows = jnp.stack([attn_bias[index, 0], zero_row, attn_bias[index, 1]])
        triple = jnp.einsum(
            "fpd,jdc->jfpc", normed, attn_full[index], preferred_element_type=jnp.float32
        )
        triple = (triple + bias_rows[:, None, None, :]).astype(jnp.bfloat16)
        if temporal:
            triple = lax.all_to_all(triple, "ctx", split_axis=2, concat_axis=1, tiled=True)
        mixed, log_total = attend(triple, temporal)
        if temporal:
            mixed = lax.all_to_all(mixed, "ctx", split_axis=0, concat_axis=1, tiled=True)
        partial_out = jnp.einsum(
            "fpc,cd->fpd", mixed, out_full[index], preferred_element_type=jnp.float32
        )
        stream_next = stream + (sum_rows(partial_out) + out_bias[index])
        return (stream_next, (normed, triple, log_total, mixed))

    def attn_backward(stream, index, weights_all, kept, grad_stream, temporal):
        attn_full, out_full = (weights_all[0], weights_all[1])
        normed, triple, log_total, mixed = kept
        grad_branch = grad_stream.astype(jnp.bfloat16)
        grad_bias_out = jnp.sum(grad_branch.astype(jnp.float32), axis=(0, 1))
        grad_full = spread_grads(grad_branch)
        grad_weight_out = jnp.einsum(
            "fpc,fpd->cd", mixed, grad_full, preferred_element_type=jnp.float32
        )
        grad_mixed = jnp.einsum(
            "fpd,cd->fpc", grad_full, out_full[index], preferred_element_type=jnp.float32
        ).astype(jnp.bfloat16)
        if temporal:
            grad_mixed = lax.all_to_all(grad_mixed, "ctx", split_axis=1, concat_axis=0, tiled=True)
        grad_triple = attend_back(triple, log_total, grad_mixed, temporal)
        if temporal:
            grad_triple = lax.all_to_all(
                grad_triple, "ctx", split_axis=1, concat_axis=2, tiled=True
            )
        grad_weight_attn = jnp.einsum(
            "fpd,jfpc->jdc", normed, grad_triple, preferred_element_type=jnp.float32
        )
        column_sums = jnp.sum(grad_triple.astype(jnp.float32), axis=(1, 2))
        grad_bias_attn = jnp.stack([column_sums[0], column_sums[2]])
        grad_normed = sum_grads(
            jnp.einsum(
                "jfpc,jdc->fpd", grad_triple, attn_full[index], preferred_element_type=jnp.float32
            )
        )
        unused, pull = jax.vjp(layer_norm, stream, norm_gain[index], norm_bias[index])
        grad_input, grad_gain, grad_shift = pull(grad_normed)
        return (
            grad_stream + grad_input,
            (
                grad_gain,
                grad_shift,
                grad_weight_attn,
                grad_bias_attn,
                grad_weight_out,
                grad_bias_out,
            ),
        )

    def mlp_forward(stream, weights_all):
        up_full, down_full = (weights_all[2], weights_all[3])
        normed = layer_norm(stream, norm_gain[2], norm_bias[2]).astype(jnp.bfloat16)
        normed = spread_rows(normed)
        hidden = (
            jnp.einsum("fpd,dc->fpc", normed, up_full, preferred_element_type=jnp.float32)
            + up_bias_used
        )
        active = gelu_exact(hidden).astype(jnp.bfloat16)
        partial_out = jnp.einsum(
            "fpc,cd->fpd", active, down_full, preferred_element_type=jnp.float32
        )
        partial_out = sum_rows(partial_out)
        return (stream + (partial_out + down_bias), (normed, hidden, active))

    def mlp_backward(stream, weights_all, kept, grad_stream):
        up_full, down_full = (weights_all[2], weights_all[3])
        normed, hidden, active = kept
        grad_branch = grad_stream.astype(jnp.bfloat16)
        grad_bias_down = jnp.sum(grad_branch.astype(jnp.float32), axis=(0, 1))
        grad_full = spread_grads(grad_branch)
        grad_weight_down = jnp.einsum(
            "fpc,fpd->cd", active, grad_full, preferred_element_type=jnp.float32
        )
        grad_active = jnp.einsum(
            "fpd,cd->fpc", grad_full, down_full, preferred_element_type=jnp.float32
        )
        unused, pull_gelu = jax.vjp(gelu_exact, hidden)
        grad_hidden = pull_gelu(grad_active)[0].astype(jnp.bfloat16)
        grad_bias_up = jnp.sum(grad_hidden.astype(jnp.float32), axis=(0, 1))
        grad_weight_up = jnp.einsum(
            "fpd,fpc->dc", normed, grad_hidden, preferred_element_type=jnp.float32
        )
        grad_normed = jnp.einsum(
            "fpc,dc->fpd", grad_hidden, up_full, preferred_element_type=jnp.float32
        )
        grad_normed = sum_grads(grad_normed)
        unused_ln, pull = jax.vjp(layer_norm, stream, norm_gain[2], norm_bias[2])
        grad_input, grad_gain, grad_shift = pull(grad_normed)
        return (
            grad_stream + grad_input,
            (grad_gain, grad_shift, grad_weight_up, grad_bias_up, grad_weight_down, grad_bias_down),
        )

    def step(totals, pair):
        clip, grad_clip = pair
        forward_weights = fetch_weights()
        backward_weights = fetch_weights()
        stream_first = clip.astype(jnp.float32)
        stream_second, kept_spatial = attn_forward(stream_first, 0, forward_weights, False)
        stream_third, kept_temporal = attn_forward(stream_second, 1, forward_weights, True)
        result, kept_mlp = mlp_forward(stream_third, forward_weights)
        grad_third, mlp_terms = mlp_backward(
            stream_third, backward_weights, kept_mlp, grad_clip.astype(jnp.float32)
        )
        grad_second, temporal_terms = attn_backward(
            stream_second, 1, backward_weights, kept_temporal, grad_third, True
        )
        grad_first, spatial_terms = attn_backward(
            stream_first, 0, backward_weights, kept_spatial, grad_second, False
        )
        increments = (
            jnp.stack([spatial_terms[0], temporal_terms[0], mlp_terms[0]]),
            jnp.stack([spatial_terms[1], temporal_terms[1], mlp_terms[1]]),
            jnp.stack([spatial_terms[2], temporal_terms[2]]),
            jnp.stack([spatial_terms[3], temporal_terms[3]]),
            jnp.stack([spatial_terms[4], temporal_terms[4]]),
            jnp.stack([spatial_terms[5], temporal_terms[5]]),
            mlp_terms[2],
            mlp_terms[3],
            mlp_terms[4],
            mlp_terms[5],
        )
        totals = jax.tree.map(jnp.add, totals, increments)
        return (totals, (result.astype(jnp.bfloat16), grad_first.astype(jnp.bfloat16)))

    start = (
        jnp.zeros((3, model_width), jnp.float32),
        jnp.zeros((3, model_width), jnp.float32),
        jnp.zeros((2, 3, model_width, width), jnp.float32),
        jnp.zeros((2, 2, width), jnp.float32),
        jnp.zeros((2, width, model_width), jnp.float32),
        jnp.zeros((2, model_width), jnp.float32),
        jnp.zeros((model_width, used_hidden), jnp.float32),
        jnp.zeros((used_hidden,), jnp.float32),
        jnp.zeros((used_hidden, model_width), jnp.float32),
        jnp.zeros((model_width,), jnp.float32),
    )
    totals, stacked = lax.scan(step, start, (inputs, cotangent))
    up_total, down_total = (totals[6], totals[8])
    up_bias_full = lax.dynamic_update_slice_in_dim(
        jnp.zeros((hidden_width * lax.axis_size("tp"),), jnp.float32),
        totals[7],
        tp_rank * hidden_width,
        0,
    )
    matrices = (
        lax.psum_scatter(totals[2], ("fsdp", "ctx"), scatter_dimension=2, tiled=True),
        lax.psum_scatter(totals[4], ("fsdp", "ctx"), scatter_dimension=2, tiled=True),
        lax.psum_scatter(up_total, ("fsdp", "ctx"), scatter_dimension=0, tiled=True),
        lax.psum_scatter(down_total, ("fsdp", "ctx"), scatter_dimension=1, tiled=True),
    )
    attn_bias_full = lax.dynamic_update_slice_in_dim(
        jnp.zeros((2, 2, model_width), jnp.float32), totals[3], tp_rank * width, 2
    )
    vectors = lax.psum(
        (totals[0], totals[1], attn_bias_full, totals[5], up_bias_full, totals[9]),
        ("fsdp", "ctx", "tp"),
    )
    attn_bias_part = lax.dynamic_slice_in_dim(vectors[2], tp_rank * width, width, 2)
    return (
        stacked[0],
        stacked[1],
        vectors[0],
        vectors[1],
        matrices[0],
        attn_bias_part,
        matrices[1],
        vectors[3],
        matrices[2],
        vectors[4],
        matrices[3],
        vectors[5],
    )


def solution(mesh):
    return jax.shard_map(
        local,
        mesh=mesh,
        in_specs=(
            P("fsdp", "ctx", "tp", None),
            P("fsdp", "ctx", "tp", None),
            P(),
            P(),
            P(None, None, "fsdp", "tp"),
            P(None, None, "tp"),
            P(None, "tp", "fsdp"),
            P(),
            P("fsdp", "tp"),
            P(),
            P("tp", "fsdp"),
            P(),
        ),
        out_specs=(
            P("fsdp", "ctx", "tp", None),
            P("fsdp", "ctx", "tp", None),
            P(),
            P(),
            P(None, None, ("fsdp", "ctx"), "tp"),
            P(None, None, "tp"),
            P(None, "tp", ("fsdp", "ctx")),
            P(),
            P(("fsdp", "ctx"), "tp"),
            P(),
            P("tp", ("fsdp", "ctx")),
            P(),
        ),
        check_vma=False,
    )
```

profile of v0, /device:TPU:0, one launch (start us, length us, event | category | flops | bytes accessed | tf_op | source)
XLA Modules:
  0.0 1763.9 jit_solution(5922801304353576764)
XLA Ops:
  9.5 1556.3 %while.33 = (s32[]{:T(128)}, f32[3,768]{1,0:T(4,128)}, f32[3,768]{1,0:T(4,128)}, f32[2,3,768,192]{2,3,1,0:T(8,128)}, f32[2,2,192]{2,1,0:T(2,128)}, /*index=5*/f3...) while((s32[]{:T(128)}, f32[3,768]{1,0:T(4,128)}, ...), condition=%wide.region_37.0_spmd.clone, body=%wide.region_0.37_spmd.clone.sunk | while | flops 11599428608 | bytes 431165984 | solution.py:273
  16.3 14.6 all_gather.55
  30.9 15.2 all-gather.18.cloned.1.call-done
  46.1 34.4 %all-gather.16.cloned.1.call-done = bf16[4,196,768]{2,0,1:T(4,128)(2,1)} async-done(((bf16[4,49,768]{2,0,1:T(4,128)(2,1)}), bf16[4,196,768]{2,0,1:T(4,128)(2,1)}) %all-gather.16.cloned.1.call-update) | async-done | bytes 1204240 | tf_op jit(solution)/shard_map/while/body/eval_jaxpr/all_gather | solution.py:105
  89.9 54.9 %all-reduce.24.cloned.1.call-done = bf16[4,196,768]{2,0,1:T(4,128)(2,1)} async-done(((bf16[4,196,768]{2,0,1:T(4,128)(2,1)}), bf16[4,196,768]{2,0,1:T(4,128)(2,1)}) %all-reduce.24.cloned.1.call-update) | async-done | bytes 1204240 | tf_op jit(solution)/shard_map/while
  149.7 30.2 %all-gather.20.cloned.1.call-done = bf16[4,196,768]{2,0,1:T(4,128)(2,1)} async-done(((bf16[4,49,768]{2,0,1:T(4,128)(2,1)}), bf16[4,196,768]{2,0,1:T(4,128)(2,1)}) %all-gather.20.cloned.1.call-update) | async-done | bytes 1204240 | tf_op jit(solution)/shard_map/while/body/eval_jaxpr/all_gather | solution.py:105
  179.9 3.7 fusion.237
  183.6 3.5 copy.354
  187.1 20.1 %all_to_all.74 = bf16[3,4,196,192]{3,1,0,2:T(4,128)(2,1)S(1)} all-to-all(bf16[3,4,196,192]{3,1,0,2:T(4,128)(2,1)} %copy.354), channel_id=1, replica_groups=mesh['fsdp'=2,'ctx'=4,'tp'=4] {'ctx'}, dimensions={2} | all-to-all | bytes 1806336 | tf_op jit(solution)/shard_map/while/body/eval_jaxpr/all_to_all | solution.py:132
  227.6 11.7 all_to_all.75
  245.9 54.7 %all-reduce.26.cloned.1.call-done = bf16[4,196,768]{2,0,1:T(4,128)(2,1)} async-done(((bf16[4,196,768]{2,0,1:T(4,128)(2,1)}), bf16[4,196,768]{2,0,1:T(4,128)(2,1)}) %all-reduce.26.cloned.1.call-update) | async-done | bytes 1204240 | tf_op jit(solution)/shard_map/while
  306.5 17.8 %all-gather.14.cloned.1.call-done = bf16[768,768]{1,0:T(8,128)(2,1)} async-done(((bf16[384,768]{1,0:T(8,128)(2,1)}), bf16[768,768]{1,0:T(8,128)(2,1)}) %all-gather.14.cloned.1.call-update) | async-done | bytes 1179664 | tf_op jit(solution)/shard_map/while/body/eval_jaxpr/all_gather | solution.py:100
  324.3 32.9 %all-gather.22.cloned.1.call-done = bf16[4,196,768]{2,0,1:T(4,128)(2,1)} async-done(((bf16[4,49,768]{2,0,1:T(4,128)(2,1)}), bf16[4,196,768]{2,0,1:T(4,128)(2,1)}) %all-gather.22.cloned.1.call-update) | async-done | bytes 1204240 | tf_op jit(solution)/shard_map/while/body/eval_jaxpr/all_gather | solution.py:105
  357.2 3.3 fusion.243
  361.9 6.8 multiply_convert_fusion.6
  368.7 12.0 all-gather.24.cloned.1.call-done
  380.7 32.3 %all-gather.26.cloned.1.call-done = bf16[1,4,196,768]{3,1,0,2:T(4,128)(2,1)} async-done(((bf16[1,4,49,768]{3,1,0,2:T(4,128)(2,1)}), bf16[1,4,196,768]{3,1,0,2:T(4,128)(2,1)}) %all-gather.26.cloned.1.call-update) | async-done | bytes 1204240 | tf_op jit(solution)/shard_map/while/body/eval_jaxpr/all_gather | solution.py:113
  413.0 5.7 convert_reduce_fusion.20
  421.4 56.2 %all-reduce.28.cloned.1.call-done = bf16[4,196,768]{2,0,1:T(4,128)(2,1)} async-done(((bf16[4,196,768]{2,0,1:T(4,128)(2,1)}), bf16[4,196,768]{2,0,1:T(4,128)(2,1)}) %all-reduce.28.cloned.1.call-update) | async-done | bytes 1204240 | tf_op jit(solution)/shard_map/while
  485.1 30.2 %all-gather.28.cloned.1.call-done = bf16[4,196,768]{2,0,1:T(4,128)(2,1)} async-done(((bf16[4,49,768]{2,0,1:T(4,128)(2,1)}), bf16[4,196,768]{2,0,1:T(4,128)(2,1)}) %all-gather.28.cloned.1.call-update) | async-done | bytes 1204240 | tf_op jit(solution)/shard_map/while/body/eval_jaxpr/all_gather | solution.py:113
  520.0 11.1 all_to_all.76
  555.3 20.4 %all_to_all.77 = bf16[3,16,49,192]{3,2,0,1:T(8,128)(2,1)S(1)} all-to-all(bf16[3,16,49,192]{3,2,0,1:T(8,128)(2,1)S(1)} %copy.369), channel_id=1, replica_groups=mesh['fsdp'=2,'ctx'=4,'tp'=4] {'ctx'}, dimensions={1} | all-to-all | bytes 1806336 | tf_op jit(solution)/shard_map/while/body/eval_jaxpr/all_to_all | solution.py:158
  582.6 3.8 convolution_convert_fusion.25
  586.4 49.8 %all-reduce.30.cloned.1.call-done = bf16[4,196,768]{2,0,1:T(4,128)(2,1)} async-done(((bf16[4,196,768]{2,0,1:T(4,128)(2,1)}), bf16[4,196,768]{2,0,1:T(4,128)(2,1)}) %all-reduce.30.cloned.1.call-update) | async-done | bytes 1204240 | tf_op jit(solution)/shard_map/while
  641.4 3.7 convert_reduce_fusion.24
  648.7 3.9 bitcast_add_fusion.4
  657.8 17.7 %all-gather.30.cloned.1.call-done = bf16[4,196,768]{2,0,1:T(4,128)(2,1)} async-done(((bf16[4,49,768]{2,0,1:T(4,128)(2,1)}), bf16[4,196,768]{2,0,1:T(4,128)(2,1)}) %all-gather.30.cloned.1.call-update) | async-done | bytes 1204240 | tf_op jit(solution)/shard_map/while/body/eval_jaxpr/all_gather | solution.py:113
  685.2 3.0 convolution_bitcast_fusion.8
  694.8 86.4 %all-reduce.32.cloned.1.call-done = (bf16[4,196,768]{2,0,1:T(4,128)(2,1)}, bf16[4,196,768]{2,0,1:T(4,128)(2,1)}) async-done(((bf16[4,196,768]{2,0,1:T(4,128)(2,1)}, bf16[4,196,768]{2,0,1:T(4,128)(2,1)}), (bf16[4,196,768]{2,0,1:T(4,128)(2,1)}, bf16[4,196,768]{2,0,1:T(4,128)(2,1)})) %all-reduce.32.cloned.1.call-update) | async-done | bytes 2408464 | tf_op jit(solution)/shard_map/while
  794.5 15.3 all_gather.55
  809.9 13.1 all-gather.18.cloned.1.call-done
  822.9 31.8 %all-gather.16.cloned.1.call-done = bf16[4,196,768]{2,0,1:T(4,128)(2,1)} async-done(((bf16[4,49,768]{2,0,1:T(4,128)(2,1)}), bf16[4,196,768]{2,0,1:T(4,128)(2,1)}) %all-gather.16.cloned.1.call-update) | async-done | bytes 1204240 | tf_op jit(solution)/shard_map/while/body/eval_jaxpr/all_gather | solution.py:105
  864.2 54.9 %all-reduce.24.cloned.1.call-done = bf16[4,196,768]{2,0,1:T(4,128)(2,1)} async-done(((bf16[4,196,768]{2,0,1:T(4,128)(2,1)}), bf16[4,196,768]{2,0,1:T(4,128)(2,1)}) %all-reduce.24.cloned.1.call-update) | async-done | bytes 1204240 | tf_op jit(solution)/shard_map/while
  924.0 30.2 %all-gather.20.cloned.1.call-done = bf16[4,196,768]{2,0,1:T(4,128)(2,1)} async-done(((bf16[4,49,768]{2,0,1:T(4,128)(2,1)}), bf16[4,196,768]{2,0,1:T(4,128)(2,1)}) %all-gather.20.cloned.1.call-update) | async-done | bytes 1204240 | tf_op jit(solution)/shard_map/while/body/eval_jaxpr/all_gather | solution.py:105
  954.2 3.7 fusion.237
  957.9 3.5 copy.354
  961.3 19.8 %all_to_all.74 = bf16[3,4,196,192]{3,1,0,2:T(4,128)(2,1)S(1)} all-to-all(bf16[3,4,196,192]{3,1,0,2:T(4,128)(2,1)} %copy.354), channel_id=1, replica_groups=mesh['fsdp'=2,'ctx'=4,'tp'=4] {'ctx'}, dimensions={2} | all-to-all | bytes 1806336 | tf_op jit(solution)/shard_map/while/body/eval_jaxpr/all_to_all | solution.py:132
  1001.7 11.7 all_to_all.75
  1020.0 54.7 %all-reduce.26.cloned.1.call-done = bf16[4,196,768]{2,0,1:T(4,128)(2,1)} async-done(((bf16[4,196,768]{2,0,1:T(4,128)(2,1)}), bf16[4,196,768]{2,0,1:T(4,128)(2,1)}) %all-reduce.26.cloned.1.call-update) | async-done | bytes 1204240 | tf_op jit(solution)/shard_map/while
  1080.8 17.5 all-gather.14.cloned.1.call-done
  1098.4 32.9 %all-gather.22.cloned.1.call-done = bf16[4,196,768]{2,0,1:T(4,128)(2,1)} async-done(((bf16[4,49,768]{2,0,1:T(4,128)(2,1)}), bf16[4,196,768]{2,0,1:T(4,128)(2,1)}) %all-gather.22.cloned.1.call-update) | async-done | bytes 1204240 | tf_op jit(solution)/shard_map/while/body/eval_jaxpr/all_gather | solution.py:105
  1131.2 3.3 fusion.243
  1136.0 6.8 multiply_convert_fusion.6
  1142.7 12.0 all-gather.24.cloned.1.call-done
  1154.8 32.3 %all-gather.26.cloned.1.call-done = bf16[1,4,196,768]{3,1,0,2:T(4,128)(2,1)} async-done(((bf16[1,4,49,768]{3,1,0,2:T(4,128)(2,1)}), bf16[1,4,196,768]{3,1,0,2:T(4,128)(2,1)}) %all-gather.26.cloned.1.call-update) | async-done | bytes 1204240 | tf_op jit(solution)/shard_map/while/body/eval_jaxpr/all_gather | solution.py:113
  1187.1 5.7 convert_reduce_fusion.20
  1195.5 56.2 %all-reduce.28.cloned.1.call-done = bf16[4,196,768]{2,0,1:T(4,128)(2,1)} async-done(((bf16[4,196,768]{2,0,1:T(4,128)(2,1)}), bf16[4,196,768]{2,0,1:T(4,128)(2,1)}) %all-reduce.28.cloned.1.call-update) | async-done | bytes 1204240 | tf_op jit(solution)/shard_map/while
  1259.1 30.2 %all-gather.28.cloned.1.call-done = bf16[4,196,768]{2,0,1:T(4,128)(2,1)} async-done(((bf16[4,49,768]{2,0,1:T(4,128)(2,1)}), bf16[4,196,768]{2,0,1:T(4,128)(2,1)}) %all-gather.28.cloned.1.call-update) | async-done | bytes 1204240 | tf_op jit(solution)/shard_map/while/body/eval_jaxpr/all_gather | solution.py:113
  1294.1 11.1 all_to_all.76
  1329.3 20.4 %all_to_all.77 = bf16[3,16,49,192]{3,2,0,1:T(8,128)(2,1)S(1)} all-to-all(bf16[3,16,49,192]{3,2,0,1:T(8,128)(2,1)S(1)} %copy.369), channel_id=1, replica_groups=mesh['fsdp'=2,'ctx'=4,'tp'=4] {'ctx'}, dimensions={1} | all-to-all | bytes 1806336 | tf_op jit(solution)/shard_map/while/body/eval_jaxpr/all_to_all | solution.py:158
  1356.6 3.8 convolution_convert_fusion.25
  1360.4 49.8 %all-reduce.30.cloned.1.call-done = bf16[4,196,768]{2,0,1:T(4,128)(2,1)} async-done(((bf16[4,196,768]{2,0,1:T(4,128)(2,1)}), bf16[4,196,768]{2,0,1:T(4,128)(2,1)}) %all-reduce.30.cloned.1.call-update) | async-done | bytes 1204240 | tf_op jit(solution)/shard_map/while
  1415.5 3.7 convert_reduce_fusion.24
  1422.5 3.9 bitcast_add_fusion.4
  1431.6 17.9 %all-gather.30.cloned.1.call-done = bf16[4,196,768]{2,0,1:T(4,128)(2,1)} async-done(((bf16[4,49,768]{2,0,1:T(4,128)(2,1)}), bf16[4,196,768]{2,0,1:T(4,128)(2,1)}) %all-gather.30.cloned.1.call-update) | async-done | bytes 1204240 | tf_op jit(solution)/shard_map/while/body/eval_jaxpr/all_gather | solution.py:113
  1459.3 3.0 convolution_bitcast_fusion.8
  1466.6 4.4 maximum_add_fusion.12
  1470.9 84.3 %all-reduce.32.cloned.1.call-done = (bf16[4,196,768]{2,0,1:T(4,128)(2,1)}, bf16[4,196,768]{2,0,1:T(4,128)(2,1)}) async-done(((bf16[4,196,768]{2,0,1:T(4,128)(2,1)}, bf16[4,196,768]{2,0,1:T(4,128)(2,1)}), (bf16[4,196,768]{2,0,1:T(4,128)(2,1)}, bf16[4,196,768]{2,0,1:T(4,128)(2,1)})) %all-reduce.32.cloned.1.call-update) | async-done | bytes 2408464 | tf_op jit(solution)/shard_map/while
  1570.7 3.1 copy.196
  1574.5 5.7 copy.195
  1581.2 40.8 %all-reduce.7 = (f32[3,768]{1,0:T(4,128)}, f32[3,768]{1,0:T(4,128)}, f32[2,2,768]{2,1,0:T(2,128)S(1)}, f32[2,768]{1,0:T(2,128)}, f32[3072]{0:T(1024)}, /*index=5*/f32[768]{0:T(1024)}) all-reduce(f32[3,768]{1,0:T(4,128)S(1)} %copy-done.64, f32[3,768]{1,0:T(4,128)S(1)} %copy-done.67, ...), channel_id=1, replica_groups=mesh['fsdp'=2,'ctx'=4,'tp'=4] {'fsdp','ctx','tp'}, use_global_device_ids=true, to_apply=%region_38.0 | all-reduce | flops 13056 | bytes 104448 | tf_op jit(solution)/shard_map/psum | solution.py:290
  1624.6 27.9 %reduce-scatter.11.cloned.1.call-done = f32[768,96]{0,1:T(8,128)} async-done(((f32[768,768]{0,1:T(8,128)}), f32[768,96]{0,1:T(8,128)}) %reduce-scatter.11.cloned.1.call-update) | async-done | bytes 294928 | tf_op jit(solution)/shard_map/reduce_scatter | solution.py:285
  1652.5 46.1 %reduce-scatter.9.cloned.1.call-done = f32[96,768]{1,0:T(8,128)} async-done(((f32[768,768]{1,0:T(8,128)}), f32[96,768]{1,0:T(8,128)}) %reduce-scatter.9.cloned.1.call-update) | async-done | bytes 294928 | tf_op jit(solution)/shard_map/reduce_scatter | solution.py:284
  1698.6 57.6 %reduce-scatter.7.cloned.1.call-done = f32[2,3,96,192]{3,2,1,0:T(8,128)} async-done(((f32[2,3,768,192]{3,2,1,0:T(8,128)}), f32[2,3,96,192]{3,2,1,0:T(8,128)}) %reduce-scatter.7.cloned.1.call-update) | async-done | bytes 442384 | tf_op jit(solution)/shard_map/reduce_scatter | solution.py:282
  (718 shorter events, 280.3 us)
Async XLA Ops:
  9.5 36.6 %all-gather.18.cloned.1.call-start = ((), (), s32[]{:S(2)}) async-start(), calls=%async_computation.14 | async-start | bytes 2654208 | tf_op jit(solution)/shard_map/while/body/eval_jaxpr/all_gather | solution.py:98
  10.2 70.2 %all-gather.16.cloned.1.call-start = ((), (), s32[]{:S(2)}) async-start(), calls=%async_computation.13 | async-start | bytes 1505280 | tf_op jit(solution)/shard_map/while/body/eval_jaxpr/all_gather | solution.py:105
  12.3 70.8 %copy-start.56 = (f32[768]{0:T(1024)}, f32[768]{0:T(1024)S(1)}, u32[]{:S(2)}) copy-start(f32[768]{0:T(1024)S(1)} %get-tuple-element.657) | copy-start | bytes 9220 | tf_op jit(solution)/shard_map/while
  12.3 135.2 %copy-start.54 = (f32[768]{0:T(1024)}, f32[768]{0:T(1024)S(1)}, u32[]{:S(2)}) copy-start(f32[768]{0:T(1024)S(1)} %get-tuple-element.649) | copy-start | bytes 9220 | tf_op jit(solution)/shard_map/while
  15.1 68.1 %copy-start.50 = (f32[4,49]{0,1:T(8,128)}, f32[4,49]{0,1:T(8,128)S(1)}, u32[]{:S(2)}) copy-start(f32[4,49]{0,1:T(8,128)S(1)} %fusion.230) | copy-start | bytes 2356 | tf_op jit(solution)/shard_map/while
  15.1 68.0 %copy-start.39 = (f32[4,49]{0,1:T(8,128)}, f32[4,49]{0,1:T(8,128)S(1)}, u32[]{:S(2)}) copy-start(f32[4,49]{0,1:T(8,128)S(1)} %fusion.231) | copy-start | bytes 2356 | tf_op jit(solution)/shard_map/while
  16.2 128.7 %all-reduce.24.cloned.1.call-start = ((), (), s32[]{:S(2)}) async-start(), calls=%async_computation.15 | async-start | bytes 2408448 | tf_op jit(solution)/shard_map/while
  88.6 91.4 %all-gather.20.cloned.1.call-start = ((), (), s32[]{:S(2)}) async-start(), calls=%async_computation.16 | async-start | bytes 1505280 | tf_op jit(solution)/shard_map/while/body/eval_jaxpr/all_gather | solution.py:105
  149.6 151.0 %all-reduce.26.cloned.1.call-start = ((), (), s32[]{:S(2)}) async-start(), calls=%async_computation.17 | async-start | bytes 2408448 | tf_op jit(solution)/shard_map/while
  245.3 57.3 %copy-start.74 = (f32[768]{0:T(1024)S(1)}, f32[768]{0:T(1024)}, u32[]{:S(2)}) copy-start(f32[768]{0:T(1024)} %get-tuple-element.670) | copy-start | bytes 9220 | tf_op jit(solution)/shard_map/while
  245.3 79.0 %all-gather.14.cloned.1.call-start = ((), (), s32[]{:S(2)}) async-start(), calls=%async_computation.12 | async-start | bytes 1769472 | tf_op jit(solution)/shard_map/while/body/eval_jaxpr/all_gather | solution.py:100
  245.9 111.3 %all-gather.22.cloned.1.call-start = ((), (), s32[]{:S(2)}) async-start(), calls=%async_computation.18 | async-start | bytes 1505280 | tf_op jit(solution)/shard_map/while/body/eval_jaxpr/all_gather | solution.py:105
  302.6 179.5 %copy-start.36 = (f32[4,49]{0,1:T(8,128)}, f32[4,49]{0,1:T(8,128)S(1)}, u32[]{:S(2)}) copy-start(f32[4,49]{0,1:T(8,128)S(1)} %fusion.242) | copy-start | bytes 2356 | tf_op jit(solution)/shard_map/while
  303.6 77.1 %all-gather.24.cloned.1.call-start = ((), (), s32[]{:S(2)}) async-start(), calls=%async_computation.19 | async-start | bytes 1769472 | tf_op jit(solution)/shard_map/while/body/eval_jaxpr/all_gather | solution.py:101
  304.4 108.6 %all-gather.26.cloned.1.call-start = ((), (), s32[]{:S(2)}) async-start(), calls=%async_computation.20 | async-start | bytes 1505280 | tf_op jit(solution)/shard_map/while/body/eval_jaxpr/all_gather | solution.py:113
  306.3 171.4 %all-reduce.28.cloned.1.call-start = ((), (), s32[]{:S(2)}) async-start(), calls=%async_computation.21 | async-start | bytes 2408448 | tf_op jit(solution)/shard_map/while
  421.3 94.0 %all-gather.28.cloned.1.call-start = ((), (), s32[]{:S(2)}) async-start(), calls=%async_computation.22 | async-start | bytes 1505280 | tf_op jit(solution)/shard_map/while/body/eval_jaxpr/all_gather | solution.py:113
  485.0 151.1 %all-reduce.30.cloned.1.call-start = ((), (), s32[]{:S(2)}) async-start(), calls=%async_computation.23 | async-start | bytes 2408448 | tf_op jit(solution)/shard_map/while
  580.8 94.7 %all-gather.30.cloned.1.call-start = ((), (), s32[]{:S(2)}) async-start(), calls=%async_computation.24 | async-start | bytes 1505280 | tf_op jit(solution)/shard_map/while/body/eval_jaxpr/all_gather | solution.py:113
  582.6 56.0 %copy-start.53 = (f32[4,49]{0,1:T(8,128)S(1)}, f32[4,49]{0,1:T(8,128)}, u32[]{:S(2)}) copy-start(f32[4,49]{0,1:T(8,128)} %copy-done.52) | copy-start | bytes 2356 | tf_op jit(solution)/shard_map/while
  582.6 56.0 %copy-start.42 = (f32[4,49]{0,1:T(8,128)S(1)}, f32[4,49]{0,1:T(8,128)}, u32[]{:S(2)}) copy-start(f32[4,49]{0,1:T(8,128)} %copy-done.41) | copy-start | bytes 2356 | tf_op jit(solution)/shard_map/while
  586.4 55.0 %copy-start.44 = (f32[4,49]{0,1:T(8,128)S(1)}, f32[4,49]{0,1:T(8,128)}, u32[]{:S(2)}) copy-start(f32[4,49]{0,1:T(8,128)} %copy-done.43) | copy-start | bytes 2356 | tf_op jit(solution)/shard_map/while
  586.4 55.0 %copy-start.49 = (f32[4,49]{0,1:T(8,128)S(1)}, f32[4,49]{0,1:T(8,128)}, u32[]{:S(2)}) copy-start(f32[4,49]{0,1:T(8,128)} %copy-done.48) | copy-start | bytes 2356 | tf_op jit(solution)/shard_map/while
  645.2 136.0 %all-reduce.32.cloned.1.call-start = ((), (), s32[]{:S(2)}) async-start(), calls=%async_computation.25 | async-start | bytes 4816896 | tf_op jit(solution)/shard_map/while
  692.5 88.7 %copy-start.4 = (bf16[2,4,49,768]{3,1,2,0:T(4,128)(2,1)S(1)}, bf16[2,4,49,768]{3,1,2,0:T(4,128)(2,1)}, u32[]{:S(2)}) copy-start(bf16[2,4,49,768]{3,1,2,0:T(4,128)(2,1)} %get-tuple-element.787) | copy-start | bytes 1806340 | tf_op jit(solution)/shard_map/while
  692.5 88.7 %copy-start.57 = (f32[768]{0:T(1024)S(1)}, f32[768]{0:T(1024)}, u32[]{:S(2)}) copy-start(f32[768]{0:T(1024)} %copy-done.56) | copy-start | bytes 9220 | tf_op jit(solution)/shard_map/while
  692.5 90.1 %copy-start.51 = (f32[4,49]{0,1:T(8,128)S(1)}, f32[4,49]{0,1:T(8,128)}, u32[]{:S(2)}) copy-start(f32[4,49]{0,1:T(8,128)} %copy-done.50) | copy-start | bytes 2356 | tf_op jit(solution)/shard_map/while
  692.5 90.1 %copy-start.40 = (f32[4,49]{0,1:T(8,128)S(1)}, f32[4,49]{0,1:T(8,128)}, u32[]{:S(2)}) copy-start(f32[4,49]{0,1:T(8,128)} %copy-done.39) | copy-start | bytes 2356 | tf_op jit(solution)/shard_map/while
  692.5 91.9 %copy-start.89 = (f32[768]{0:T(1024)S(1)}, f32[768]{0:T(1024)}, u32[]{:S(2)}) copy-start(f32[768]{0:T(1024)} %get-tuple-element.798) | copy-start | bytes 9220 | tf_op jit(solution)/shard_map/while
  694.8 89.6 %copy-start.21 = (f32[4,49,768]{2,0,1:T(4,128)S(1)}, f32[4,49,768]{2,0,1:T(4,128)}, u32[]{:S(2)}) copy-start(f32[4,49,768]{2,0,1:T(4,128)} %get-tuple-element.706) | copy-start | bytes 1806340 | tf_op jit(solution)/shard_map/while
  787.8 35.1 %all-gather.18.cloned.1.call-start = ((), (), s32[]{:S(2)}) async-start(), calls=%async_computation.14 | async-start | bytes 2654208 | tf_op jit(solution)/shard_map/while/body/eval_jaxpr/all_gather | solution.py:98
  788.4 66.3 %all-gather.16.cloned.1.call-start = ((), (), s32[]{:S(2)}) async-start(), calls=%async_computation.13 | async-start | bytes 1505280 | tf_op jit(solution)/shard_map/while/body/eval_jaxpr/all_gather | solution.py:105
  790.5 66.9 %copy-start.56 = (f32[768]{0:T(1024)}, f32[768]{0:T(1024)S(1)}, u32[]{:S(2)}) copy-start(f32[768]{0:T(1024)S(1)} %get-tuple-element.657) | copy-start | bytes 9220 | tf_op jit(solution)/shard_map/while
  790.5 131.3 %copy-start.54 = (f32[768]{0:T(1024)}, f32[768]{0:T(1024)S(1)}, u32[]{:S(2)}) copy-start(f32[768]{0:T(1024)S(1)} %get-tuple-element.649) | copy-start | bytes 9220 | tf_op jit(solution)/shard_map/while
  793.3 64.1 %copy-start.50 = (f32[4,49]{0,1:T(8,128)}, f32[4,49]{0,1:T(8,128)S(1)}, u32[]{:S(2)}) copy-start(f32[4,49]{0,1:T(8,128)S(1)} %fusion.230) | copy-start | bytes 2356 | tf_op jit(solution)/shard_map/while
  793.3 64.1 %copy-start.39 = (f32[4,49]{0,1:T(8,128)}, f32[4,49]{0,1:T(8,128)S(1)}, u32[]{:S(2)}) copy-start(f32[4,49]{0,1:T(8,128)S(1)} %fusion.231) | copy-start | bytes 2356 | tf_op jit(solution)/shard_map/while
  794.4 124.8 %all-reduce.24.cloned.1.call-start = ((), (), s32[]{:S(2)}) async-start(), calls=%async_computation.15 | async-start | bytes 2408448 | tf_op jit(solution)/shard_map/while
  862.9 91.3 %all-gather.20.cloned.1.call-start = ((), (), s32[]{:S(2)}) async-start(), calls=%async_computation.16 | async-start | bytes 1505280 | tf_op jit(solution)/shard_map/while/body/eval_jaxpr/all_gather | solution.py:105
  923.9 150.8 %all-reduce.26.cloned.1.call-start = ((), (), s32[]{:S(2)}) async-start(), calls=%async_computation.17 | async-start | bytes 2408448 | tf_op jit(solution)/shard_map/while
  1019.3 57.3 %copy-start.74 = (f32[768]{0:T(1024)S(1)}, f32[768]{0:T(1024)}, u32[]{:S(2)}) copy-start(f32[768]{0:T(1024)} %get-tuple-element.670) | copy-start | bytes 9220 | tf_op jit(solution)/shard_map/while
  1019.4 79.0 %all-gather.14.cloned.1.call-start = ((), (), s32[]{:S(2)}) async-start(), calls=%async_computation.12 | async-start | bytes 1769472 | tf_op jit(solution)/shard_map/while/body/eval_jaxpr/all_gather | solution.py:100
  1020.0 111.3 %all-gather.22.cloned.1.call-start = ((), (), s32[]{:S(2)}) async-start(), calls=%async_computation.18 | async-start | bytes 1505280 | tf_op jit(solution)/shard_map/while/body/eval_jaxpr/all_gather | solution.py:105
  1076.6 179.5 %copy-start.36 = (f32[4,49]{0,1:T(8,128)}, f32[4,49]{0,1:T(8,128)S(1)}, u32[]{:S(2)}) copy-start(f32[4,49]{0,1:T(8,128)S(1)} %fusion.242) | copy-start | bytes 2356 | tf_op jit(solution)/shard_map/while
  1077.7 77.1 %all-gather.24.cloned.1.call-start = ((), (), s32[]{:S(2)}) async-start(), calls=%async_computation.19 | async-start | bytes 1769472 | tf_op jit(solution)/shard_map/while/body/eval_jaxpr/all_gather | solution.py:101
  1078.4 108.6 %all-gather.26.cloned.1.call-start = ((), (), s32[]{:S(2)}) async-start(), calls=%async_computation.20 | async-start | bytes 1505280 | tf_op jit(solution)/shard_map/while/body/eval_jaxpr/all_gather | solution.py:113
  1080.3 171.4 %all-reduce.28.cloned.1.call-start = ((), (), s32[]{:S(2)}) async-start(), calls=%async_computation.21 | async-start | bytes 2408448 | tf_op jit(solution)/shard_map/while
  1195.4 94.0 %all-gather.28.cloned.1.call-start = ((), (), s32[]{:S(2)}) async-start(), calls=%async_computation.22 | async-start | bytes 1505280 | tf_op jit(solution)/shard_map/while/body/eval_jaxpr/all_gather | solution.py:113
  1259.1 151.1 %all-reduce.30.cloned.1.call-start = ((), (), s32[]{:S(2)}) async-start(), calls=%async_computation.23 | async-start | bytes 2408448 | tf_op jit(solution)/shard_map/while
  1354.8 94.7 %all-gather.30.cloned.1.call-start = ((), (), s32[]{:S(2)}) async-start(), calls=%async_computation.24 | async-start | bytes 1505280 | tf_op jit(solution)/shard_map/while/body/eval_jaxpr/all_gather | solution.py:113
  1356.6 56.0 %copy-start.53 = (f32[4,49]{0,1:T(8,128)S(1)}, f32[4,49]{0,1:T(8,128)}, u32[]{:S(2)}) copy-start(f32[4,49]{0,1:T(8,128)} %copy-done.52) | copy-start | bytes 2356 | tf_op jit(solution)/shard_map/while
  1356.6 56.0 %copy-start.42 = (f32[4,49]{0,1:T(8,128)S(1)}, f32[4,49]{0,1:T(8,128)}, u32[]{:S(2)}) copy-start(f32[4,49]{0,1:T(8,128)} %copy-done.41) | copy-start | bytes 2356 | tf_op jit(solution)/shard_map/while
  1360.4 55.0 %copy-start.44 = (f32[4,49]{0,1:T(8,128)S(1)}, f32[4,49]{0,1:T(8,128)}, u32[]{:S(2)}) copy-start(f32[4,49]{0,1:T(8,128)} %copy-done.43) | copy-start | bytes 2356 | tf_op jit(solution)/shard_map/while
  1360.4 55.0 %copy-start.49 = (f32[4,49]{0,1:T(8,128)S(1)}, f32[4,49]{0,1:T(8,128)}, u32[]{:S(2)}) copy-start(f32[4,49]{0,1:T(8,128)} %copy-done.48) | copy-start | bytes 2356 | tf_op jit(solution)/shard_map/while
  1419.2 136.0 %all-reduce.32.cloned.1.call-start = ((), (), s32[]{:S(2)}) async-start(), calls=%async_computation.25 | async-start | bytes 4816896 | tf_op jit(solution)/shard_map/while
  1466.5 88.7 %copy-start.4 = (bf16[2,4,49,768]{3,1,2,0:T(4,128)(2,1)S(1)}, bf16[2,4,49,768]{3,1,2,0:T(4,128)(2,1)}, u32[]{:S(2)}) copy-start(bf16[2,4,49,768]{3,1,2,0:T(4,128)(2,1)} %get-tuple-element.787) | copy-start | bytes 1806340 | tf_op jit(solution)/shard_map/while
  1466.5 88.7 %copy-start.57 = (f32[768]{0:T(1024)S(1)}, f32[768]{0:T(1024)}, u32[]{:S(2)}) copy-start(f32[768]{0:T(1024)} %copy-done.56) | copy-start | bytes 9220 | tf_op jit(solution)/shard_map/while
  1466.5 90.1 %copy-start.51 = (f32[4,49]{0,1:T(8,128)S(1)}, f32[4,49]{0,1:T(8,128)}, u32[]{:S(2)}) copy-start(f32[4,49]{0,1:T(8,128)} %copy-done.50) | copy-start | bytes 2356 | tf_op jit(solution)/shard_map/while
  1466.5 90.1 %copy-start.40 = (f32[4,49]{0,1:T(8,128)S(1)}, f32[4,49]{0,1:T(8,128)}, u32[]{:S(2)}) copy-start(f32[4,49]{0,1:T(8,128)} %copy-done.39) | copy-start | bytes 2356 | tf_op jit(solution)/shard_map/while
  1466.6 92.0 %copy-start.89 = (f32[768]{0:T(1024)S(1)}, f32[768]{0:T(1024)}, u32[]{:S(2)}) copy-start(f32[768]{0:T(1024)} %get-tuple-element.798) | copy-start | bytes 9220 | tf_op jit(solution)/shard_map/while
  1470.9 87.6 %copy-start.21 = (f32[4,49,768]{2,0,1:T(4,128)S(1)}, f32[4,49,768]{2,0,1:T(4,128)}, u32[]{:S(2)}) copy-start(f32[4,49,768]{2,0,1:T(4,128)} %get-tuple-element.706) | copy-start | bytes 1806340 | tf_op jit(solution)/shard_map/while
  1565.8 56.9 %reduce-scatter.13.cloned.1.call-start = ((), (), s32[]{:S(2)}) async-start(), calls=%async_computation.11 | async-start | bytes 1327104
  1570.6 81.9 %reduce-scatter.11.cloned.1.call-start = ((), (), s32[]{:S(2)}) async-start(), calls=%async_computation.10 | async-start | bytes 2654208 | tf_op jit(solution)/shard_map/reduce_scatter | solution.py:285
  1573.8 124.7 %reduce-scatter.9.cloned.1.call-start = ((), (), s32[]{:S(2)}) async-start(), calls=%async_computation.9 | async-start | bytes 2654208 | tf_op jit(solution)/shard_map/reduce_scatter | solution.py:284
  1574.4 181.7 %reduce-scatter.7.cloned.1.call-start = ((), (), s32[]{:S(2)}) async-start(), calls=%async_computation.8 | async-start | bytes 5308416 | tf_op jit(solution)/shard_map/reduce_scatter | solution.py:282
  (164 other events, 1148.4 us)
Sparse Core Ops, SparseCore 0:
  11.8 34.2 all-gather.17
  48.3 32.1 all-gather.15
  88.7 56.1 all-reduce.23
  149.7 30.1 all-gather.19
  245.4 55.1 all-reduce.25
  302.1 22.2 all-gather.13
  326.4 30.6 all-gather.21
  358.7 21.9 all-gather.23
  382.3 30.6 all-gather.25
  421.5 56.1 all-reduce.27
  485.1 30.1 all-gather.27
  580.9 55.1 all-reduce.29
  645.3 30.1 all-gather.29
  685.3 95.8 all-reduce.31
  789.9 33.0 all-gather.17
  824.9 29.7 all-gather.15
  863.0 56.0 all-reduce.23
  924.0 30.1 all-gather.19
  1019.5 55.1 all-reduce.25
  1076.1 22.2 all-gather.13
  1100.5 30.6 all-gather.21
  1132.8 21.9 all-gather.23
  1156.3 30.6 all-gather.25
  1195.5 56.1 all-reduce.27
  1259.2 30.1 all-gather.27
  1355.0 55.1 all-reduce.29
  1419.4 30.1 all-gather.29
  1459.3 95.8 all-reduce.31
Sparse Core Ops, SparseCore 1:
  1570.7 35.7 reduce-scatter.12
  1610.2 42.2 reduce-scatter.10
  1656.3 42.2 reduce-scatter.8
  1702.6 53.5 reduce-scatter.6
where the time goes:
time: 1770 us; the launch traced here: 1760 us
  waiting for transfers between devices  1180 us (67%)
  blocking collectives  197 us (11%)
  local copies, waits for them, and re-layouts  154 us (9%)
  matrix products  108 us (6%)
  other arithmetic  98.1 us (6%)
    while x38, waiting for transfers between devices  606 us
    all_gather x6, waiting for transfers between devices, spread_rows(): return lax.all_gather(values, 'tp', axis=1, tiled=True)  192 us
    all_gather x6, waiting for transfers between devices, spread_grads(): return lax.all_gather(values, 'tp', axis=1, tiled=True)  161 us
    reduce_scatter x1, waiting for transfers between devices, local(): lax.psum_scatter(totals[2], ('fsdp', 'ctx'), scatter_dimension=2, tiled=T...  57.6 us
    reduce_scatter x1, waiting for transfers between devices, local(): lax.psum_scatter(up_total, ('fsdp', 'ctx'), scatter_dimension=0, tiled=True)  46.1 us
    psum x1, blocking collectives, local(): lax.psum((totals[0], totals[1], attn_bias_full, totals[5], up_bias_full,...  40.8 us
    all_to_all x2, blocking collectives, attn_backward(): lax.all_to_all(grad_triple, 'ctx', split_axis=1, concat_axis=2, tiled=True)  40.7 us
    all_to_all x2, blocking collectives, attn_forward(): lax.all_to_all(triple, 'ctx', split_axis=2, concat_axis=1, tiled=True)  39.9 us
  transfers between devices with their start and end apart: 32, of which 31 were waited for; matrix products, arithmetic and copies ran while one was open for 6% of the time, Pallas kernels for 0%

commit v1 on v0

--- a/solution.py
+++ b/solution.py
@@ -5,6 +5,27 @@
 
 HEAD = 64
 EPSILON = 1e-06
+
+
+def ring_gather(x, axis, dim):
+    length, index, extent = (lax.axis_size(axis), lax.axis_index(axis), x.shape[dim])
+    right = [(i, (i + 1) % length) for i in range(length)]
+    backward = [(i, (i - 1) % length) for i in range(length)]
+    out = jnp.zeros((*x.shape[:dim], length * extent, *x.shape[dim + 1 :]), x.dtype)
+    out = lax.dynamic_update_slice_in_dim(out, x, index * extent, axis=dim)
+    from_left = from_right = x
+    middle = length // 2
+    for step in range(1, middle + 1):
+        from_left = lax.ppermute(from_left, axis, right)
+        out = lax.dynamic_update_slice_in_dim(
+            out, from_left, (index - step) % length * extent, axis=dim
+        )
+        if step < length - middle:
+            from_right = lax.ppermute(from_right, axis, backward)
+            out = lax.dynamic_update_slice_in_dim(
+                out, from_right, (index + step) % length * extent, axis=dim
+            )
+    return out
 
 
 def layer_norm(rows, gain, shift):
@@ -110,7 +131,7 @@
         ).astype(jnp.float32)
 
     def spread_grads(values):
-        return lax.all_gather(values, "tp", axis=1, tiled=True)
+        return ring_gather(values, "tp", 1)
 
     def sum_grads(values):
         return lax.psum_scatter(

time: 1770 us -> 1730 us (0.977)
  waiting for transfers between devices: 1180 us -> 1020 us
  local copies, waits for them, and re-layouts: 154 us -> 271 us
  blocking collectives: 197 us -> 157 us
  starting transfers between devices: 2.59 us -> 35.2 us
    all_gather x6 -> x0, waiting for transfers between devices: 161 us -> none  [spread_grads(): return lax.all_gather(values, 'tp', axis=1, tiled=True)]
    dynamic_update_slice x0 -> x24, local copies, waits for them, and re-layouts: none -> 81.4 us  [the longest x12 39.1 us: ring_gather(): lax.dynamic_update_slice_in_dim(out, from_left, (index - step) % length *...]
    ppermute x0 -> x18, waiting for transfers between devices: none -> 42.9 us  [the longest x12 42.9 us: ring_gather(): from_left = lax.ppermute(from_left, axis, right)]
    all_to_all x2 -> x0, blocking collectives: 40.7 us -> none  [attn_backward(): lax.all_to_all(grad_triple, 'ctx', split_axis=1, concat_axis=2, tiled=True)]
    all_to_all x0 -> x2, waiting for transfers between devices: none -> 35.8 us  [attn_backward(): lax.all_to_all(grad_triple, 'ctx', split_axis=1, concat_axis=2, tiled=True)]
    all_gather x2, waiting for transfers between devices: 35.3 us -> 0.01 us  [fetch_weights(): lax.all_gather(up_wide, 'fsdp', axis=0, tiled=True)]
    all_gather x6, waiting for transfers between devices: 192 us -> 162 us  [spread_rows(): return lax.all_gather(values, 'tp', axis=1, tiled=True)]
    ppermute x0 -> x18, local copies, waits for them, and re-layouts: none -> 28.5 us  [the longest x12 19.5 us: ring_gather(): from_left = lax.ppermute(from_left, axis, right)]
  transfers between devices with their start and end apart: 32 -> 46, of which waited for: 31 -> 31; matrix products, arithmetic and copies ran while one was open for 6% -> 12% of each run, Pallas kernels for 0% -> 0%
where the time goes in v1:
time: 1730 us; the launch traced here: 1720 us
  waiting for transfers between devices  1020 us (59%)
  local copies, waits for them, and re-layouts  271 us (16%)
  blocking collectives  157 us (9%)
  matrix products  106 us (6%)
  other arithmetic  105 us (6%)
  starting transfers between devices  35.2 us (2%)
    while x32, waiting for transfers between devices  600 us
    all_gather x6, waiting for transfers between devices, spread_rows(): return lax.all_gather(values, 'tp', axis=1, tiled=True)  162 us
    reduce_scatter x1, waiting for transfers between devices, local(): lax.psum_scatter(totals[2], ('fsdp', 'ctx'), scatter_dimension=2, tiled=T...  57.6 us
    reduce_scatter x1, waiting for transfers between devices, local(): lax.psum_scatter(up_total, ('fsdp', 'ctx'), scatter_dimension=0, tiled=True)  46.1 us
    ppermute x12, waiting for transfers between devices, ring_gather(): from_left = lax.ppermute(from_left, axis, right)  42.9 us
    psum x1, blocking collectives, local(): lax.psum((totals[0], totals[1], attn_bias_full, totals[5], up_bias_full,...  40.8 us
    all_to_all x2, blocking collectives, attn_forward(): lax.all_to_all(triple, 'ctx', split_axis=2, concat_axis=1, tiled=True)  39.7 us
    dynamic_update_slice x12, local copies, waits for them, and re-layouts, ring_gather(): lax.dynamic_update_slice_in_dim(out, from_left, (index - step) % length *...  39.1 us
  transfers between devices with their start and end apart: 46, of which 31 were waited for; matrix products, arithmetic and copies ran while one was open for 12% of the time, Pallas kernels for 0%

profile of v1, /device:TPU:0, one launch (start us, length us, event | category | flops | bytes accessed | tf_op | source)
XLA Modules:
  0.0 1723.6 jit_solution(14047569765148558378)
XLA Ops:
  9.5 1515.9 %while.35 = (s32[]{:T(128)}, f32[3,768]{1,0:T(4,128)}, f32[3,768]{1,0:T(4,128)}, f32[2,3,768,192]{2,3,1,0:T(8,128)}, f32[2,2,192]{2,1,0:T(2,128)}, /*index=5*/f3...) while((s32[]{:T(128)}, f32[3,768]{1,0:T(4,128)}, ...), condition=%wide.region_37.38_spmd.clone, body=%wide.region_0.37_spmd.clone.sunk | while | flops 11599428608 | bytes 425757216 | solution.py:294
  16.9 15.1 all_gather.63
  32.1 14.6 all-gather.11.cloned.1.call-done
  46.7 34.4 %all-gather.9.cloned.1.call-done = bf16[4,196,768]{2,0,1:T(4,128)(2,1)} async-done(((bf16[4,49,768]{2,0,1:T(4,128)(2,1)}), bf16[4,196,768]{2,0,1:T(4,128)(2,1)}) %all-gather.9.cloned.1.call-update) | async-done | bytes 1204240 | tf_op jit(solution)/shard_map/while/body/eval_jaxpr/all_gather | solution.py:126
  90.5 54.9 %all-reduce.24.cloned.1.call-done = bf16[4,196,768]{2,0,1:T(4,128)(2,1)} async-done(((bf16[4,196,768]{2,0,1:T(4,128)(2,1)}), bf16[4,196,768]{2,0,1:T(4,128)(2,1)}) %all-reduce.24.cloned.1.call-update) | async-done | bytes 1204240 | tf_op jit(solution)/shard_map/while
  150.2 30.2 %all-gather.13.cloned.1.call-done = bf16[4,196,768]{2,0,1:T(4,128)(2,1)} async-done(((bf16[4,49,768]{2,0,1:T(4,128)(2,1)}), bf16[4,196,768]{2,0,1:T(4,128)(2,1)}) %all-gather.13.cloned.1.call-update) | async-done | bytes 1204240 | tf_op jit(solution)/shard_map/while/body/eval_jaxpr/all_gather | solution.py:126
  180.5 3.7 fusion.236
  187.6 19.9 %all_to_all.116 = bf16[3,4,196,192]{3,1,0,2:T(4,128)(2,1)S(1)} all-to-all(bf16[3,4,196,192]{3,1,0,2:T(4,128)(2,1)} %copy.348), channel_id=1, replica_groups=mesh['fsdp'=2,'ctx'=4,'tp'=4] {'ctx'}, dimensions={2} | all-to-all | bytes 1806336 | tf_op jit(solution)/shard_map/while/body/eval_jaxpr/all_to_all | solution.py:153
  227.8 11.5 all_to_all.117
  243.6 54.7 %all-reduce.26.cloned.1.call-done = bf16[4,196,768]{2,0,1:T(4,128)(2,1)} async-done(((bf16[4,196,768]{2,0,1:T(4,128)(2,1)}), bf16[4,196,768]{2,0,1:T(4,128)(2,1)}) %all-reduce.26.cloned.1.call-update) | async-done | bytes 1204240 | tf_op jit(solution)/shard_map/while
  307.0 8.1 collective-permute-done
  327.7 3.6 dynamic_update_slice.125
  333.0 3.6 dynamic_update_slice.126
  336.6 17.7 %all-gather.15.cloned.1.call-done = bf16[4,196,768]{2,0,1:T(4,128)(2,1)} async-done(((bf16[4,49,768]{2,0,1:T(4,128)(2,1)}), bf16[4,196,768]{2,0,1:T(4,128)(2,1)}) %all-gather.15.cloned.1.call-update) | async-done | bytes 1204240 | tf_op jit(solution)/shard_map/while/body/eval_jaxpr/all_gather | solution.py:126
  359.0 6.8 multiply_convert_fusion.6
  365.8 12.0 all-gather.17.cloned.1.call-done
  377.8 5.6 convert_reduce_fusion.21
  386.2 57.0 %all-reduce.28.cloned.1.call-done = bf16[4,196,768]{2,0,1:T(4,128)(2,1)} async-done(((bf16[4,196,768]{2,0,1:T(4,128)(2,1)}), bf16[4,196,768]{2,0,1:T(4,128)(2,1)}) %all-reduce.28.cloned.1.call-update) | async-done | bytes 1204240 | tf_op jit(solution)/shard_map/while
  455.1 8.3 collective-permute-done.3
  466.3 3.5 dynamic_update_slice.127
  476.3 3.6 dynamic_update_slice.129
  481.6 3.6 dynamic_update_slice.130
  489.8 11.1 all_to_all.118
  526.9 4.4 all-to-all-start.3
  531.4 17.9 %all-to-all-done.3 = bf16[3,16,49,192]{3,2,0,1:T(8,128)(2,1)} async-done(((bf16[3,16,49,192]{3,2,0,1:T(8,128)(2,1)}), bf16[3,16,49,192]{3,2,0,1:T(8,128)(2,1)}, u32[]{:S(2)}, u32[]{:S(2)}) %all-to-all-start.3) | async-done | bytes 903200 | tf_op jit(solution)/shard_map/while/body/eval_jaxpr/all_to_all | solution.py:179
  565.8 45.8 %all-reduce.30.cloned.1.call-done = bf16[4,196,768]{2,0,1:T(4,128)(2,1)} async-done(((bf16[4,196,768]{2,0,1:T(4,128)(2,1)}), bf16[4,196,768]{2,0,1:T(4,128)(2,1)}) %all-reduce.30.cloned.1.call-update) | async-done | bytes 1204240 | tf_op jit(solution)/shard_map/while
  617.5 3.8 convert_reduce_fusion.25
  628.5 5.0 collective-permute-done.6
  672.4 88.7 %all-reduce.32.cloned.1.call-done = (bf16[4,196,768]{2,0,1:T(4,128)(2,1)}, bf16[4,196,768]{2,0,1:T(4,128)(2,1)}) async-done(((bf16[4,196,768]{2,0,1:T(4,128)(2,1)}, bf16[4,196,768]{2,0,1:T(4,128)(2,1)}), (bf16[4,196,768]{2,0,1:T(4,128)(2,1)}, bf16[4,196,768]{2,0,1:T(4,128)(2,1)})) %all-reduce.32.cloned.1.call-update) | async-done | bytes 2408464 | tf_op jit(solution)/shard_map/while
  774.9 15.7 all_gather.63
  790.6 12.7 all-gather.11.cloned.1.call-done
  803.4 31.9 %all-gather.9.cloned.1.call-done = bf16[4,196,768]{2,0,1:T(4,128)(2,1)} async-done(((bf16[4,49,768]{2,0,1:T(4,128)(2,1)}), bf16[4,196,768]{2,0,1:T(4,128)(2,1)}) %all-gather.9.cloned.1.call-update) | async-done | bytes 1204240 | tf_op jit(solution)/shard_map/while/body/eval_jaxpr/all_gather | solution.py:126
  844.7 54.9 %all-reduce.24.cloned.1.call-done = bf16[4,196,768]{2,0,1:T(4,128)(2,1)} async-done(((bf16[4,196,768]{2,0,1:T(4,128)(2,1)}), bf16[4,196,768]{2,0,1:T(4,128)(2,1)}) %all-reduce.24.cloned.1.call-update) | async-done | bytes 1204240 | tf_op jit(solution)/shard_map/while
  904.5 30.2 %all-gather.13.cloned.1.call-done = bf16[4,196,768]{2,0,1:T(4,128)(2,1)} async-done(((bf16[4,49,768]{2,0,1:T(4,128)(2,1)}), bf16[4,196,768]{2,0,1:T(4,128)(2,1)}) %all-gather.13.cloned.1.call-update) | async-done | bytes 1204240 | tf_op jit(solution)/shard_map/while/body/eval_jaxpr/all_gather | solution.py:126
  934.7 3.7 fusion.236
  941.9 19.8 %all_to_all.116 = bf16[3,4,196,192]{3,1,0,2:T(4,128)(2,1)S(1)} all-to-all(bf16[3,4,196,192]{3,1,0,2:T(4,128)(2,1)} %copy.348), channel_id=1, replica_groups=mesh['fsdp'=2,'ctx'=4,'tp'=4] {'ctx'}, dimensions={2} | all-to-all | bytes 1806336 | tf_op jit(solution)/shard_map/while/body/eval_jaxpr/all_to_all | solution.py:153
  981.9 11.5 all_to_all.117
  997.8 54.7 %all-reduce.26.cloned.1.call-done = bf16[4,196,768]{2,0,1:T(4,128)(2,1)} async-done(((bf16[4,196,768]{2,0,1:T(4,128)(2,1)}), bf16[4,196,768]{2,0,1:T(4,128)(2,1)}) %all-reduce.26.cloned.1.call-update) | async-done | bytes 1204240 | tf_op jit(solution)/shard_map/while
  1061.1 8.1 collective-permute-done
  1081.6 3.6 dynamic_update_slice.125
  1087.0 3.6 dynamic_update_slice.126
  1090.5 17.7 %all-gather.15.cloned.1.call-done = bf16[4,196,768]{2,0,1:T(4,128)(2,1)} async-done(((bf16[4,49,768]{2,0,1:T(4,128)(2,1)}), bf16[4,196,768]{2,0,1:T(4,128)(2,1)}) %all-gather.15.cloned.1.call-update) | async-done | bytes 1204240 | tf_op jit(solution)/shard_map/while/body/eval_jaxpr/all_gather | solution.py:126
  1113.0 6.8 multiply_convert_fusion.6
  1119.8 12.0 all-gather.17.cloned.1.call-done
  1131.8 5.6 convert_reduce_fusion.21
  1140.1 57.1 %all-reduce.28.cloned.1.call-done = bf16[4,196,768]{2,0,1:T(4,128)(2,1)} async-done(((bf16[4,196,768]{2,0,1:T(4,128)(2,1)}), bf16[4,196,768]{2,0,1:T(4,128)(2,1)}) %all-reduce.28.cloned.1.call-update) | async-done | bytes 1204240 | tf_op jit(solution)/shard_map/while
  1209.1 8.3 collective-permute-done.3
  1220.3 3.5 dynamic_update_slice.127
  1230.3 3.6 dynamic_update_slice.129
  1235.6 3.6 dynamic_update_slice.130
  1243.8 11.1 all_to_all.118
  1280.9 4.4 all-to-all-start.3
  1285.4 17.9 %all-to-all-done.3 = bf16[3,16,49,192]{3,2,0,1:T(8,128)(2,1)} async-done(((bf16[3,16,49,192]{3,2,0,1:T(8,128)(2,1)}), bf16[3,16,49,192]{3,2,0,1:T(8,128)(2,1)}, u32[]{:S(2)}, u32[]{:S(2)}) %all-to-all-start.3) | async-done | bytes 903200 | tf_op jit(solution)/shard_map/while/body/eval_jaxpr/all_to_all | solution.py:179
  1315.1 5.4 bitcast_add_fusion.4
  1322.3 43.3 %all-reduce.30.cloned.1.call-done = bf16[4,196,768]{2,0,1:T(4,128)(2,1)} async-done(((bf16[4,196,768]{2,0,1:T(4,128)(2,1)}), bf16[4,196,768]{2,0,1:T(4,128)(2,1)}) %all-reduce.30.cloned.1.call-update) | async-done | bytes 1204240 | tf_op jit(solution)/shard_map/while
  1371.5 3.8 convert_reduce_fusion.25
  1382.5 5.0 collective-permute-done.6
  1424.0 4.4 maximum_add_fusion.12
  1428.4 86.6 %all-reduce.32.cloned.1.call-done = (bf16[4,196,768]{2,0,1:T(4,128)(2,1)}, bf16[4,196,768]{2,0,1:T(4,128)(2,1)}) async-done(((bf16[4,196,768]{2,0,1:T(4,128)(2,1)}, bf16[4,196,768]{2,0,1:T(4,128)(2,1)}), (bf16[4,196,768]{2,0,1:T(4,128)(2,1)}, bf16[4,196,768]{2,0,1:T(4,128)(2,1)})) %all-reduce.32.cloned.1.call-update) | async-done | bytes 2408464 | tf_op jit(solution)/shard_map/while
  1534.1 5.7 copy.207
  1540.8 40.8 %all-reduce.7 = (f32[3,768]{1,0:T(4,128)}, f32[3,768]{1,0:T(4,128)}, f32[2,2,768]{2,1,0:T(2,128)S(1)}, f32[2,768]{1,0:T(2,128)}, f32[3072]{0:T(1024)}, /*index=5*/f32[768]{0:T(1024)}) all-reduce(f32[3,768]{1,0:T(4,128)S(1)} %copy-done.64, f32[3,768]{1,0:T(4,128)S(1)} %copy-done.67, ...), channel_id=1, replica_groups=mesh['fsdp'=2,'ctx'=4,'tp'=4] {'fsdp','ctx','tp'}, use_global_device_ids=true, to_apply=%region_38.39 | all-reduce | flops 13056 | bytes 104448 | tf_op jit(solution)/shard_map/psum | solution.py:311
  1584.2 27.9 %reduce-scatter.11.cloned.1.call-done = f32[768,96]{0,1:T(8,128)} async-done(((f32[768,768]{0,1:T(8,128)}), f32[768,96]{0,1:T(8,128)}) %reduce-scatter.11.cloned.1.call-update) | async-done | bytes 294928 | tf_op jit(solution)/shard_map/reduce_scatter | solution.py:306
  1612.1 46.1 %reduce-scatter.9.cloned.1.call-done = f32[96,768]{1,0:T(8,128)} async-done(((f32[768,768]{1,0:T(8,128)}), f32[96,768]{1,0:T(8,128)}) %reduce-scatter.9.cloned.1.call-update) | async-done | bytes 294928 | tf_op jit(solution)/shard_map/reduce_scatter | solution.py:305
  1658.2 57.6 %reduce-scatter.7.cloned.1.call-done = f32[2,3,96,192]{3,2,1,0:T(8,128)} async-done(((f32[2,3,768,192]{3,2,1,0:T(8,128)}), f32[2,3,96,192]{3,2,1,0:T(8,128)}) %reduce-scatter.7.cloned.1.call-update) | async-done | bytes 442384 | tf_op jit(solution)/shard_map/reduce_scatter | solution.py:303
  (802 shorter events, 421.1 us)
Async XLA Ops:
  9.5 37.2 %all-gather.11.cloned.1.call-start = ((), (), s32[]{:S(2)}) async-start(), calls=%async_computation.14 | async-start | bytes 2654208 | tf_op jit(solution)/shard_map/while/body/eval_jaxpr/all_gather | solution.py:119
  10.2 70.8 %all-gather.9.cloned.1.call-start = ((), (), s32[]{:S(2)}) async-start(), calls=%async_computation.13 | async-start | bytes 1505280 | tf_op jit(solution)/shard_map/while/body/eval_jaxpr/all_gather | solution.py:126
  12.9 70.8 %copy-start.58 = (f32[768]{0:T(1024)}, f32[768]{0:T(1024)S(1)}, u32[]{:S(2)}) copy-start(f32[768]{0:T(1024)S(1)} %get-tuple-element.842) | copy-start | bytes 9220 | tf_op jit(solution)/shard_map/while
  12.9 135.2 %copy-start.56 = (f32[768]{0:T(1024)}, f32[768]{0:T(1024)S(1)}, u32[]{:S(2)}) copy-start(f32[768]{0:T(1024)S(1)} %get-tuple-element.834) | copy-start | bytes 9220 | tf_op jit(solution)/shard_map/while
  15.6 68.1 %copy-start.50 = (f32[4,49]{0,1:T(8,128)}, f32[4,49]{0,1:T(8,128)S(1)}, u32[]{:S(2)}) copy-start(f32[4,49]{0,1:T(8,128)S(1)} %fusion.229) | copy-start | bytes 2356 | tf_op jit(solution)/shard_map/while
  15.7 68.0 %copy-start.39 = (f32[4,49]{0,1:T(8,128)}, f32[4,49]{0,1:T(8,128)S(1)}, u32[]{:S(2)}) copy-start(f32[4,49]{0,1:T(8,128)S(1)} %fusion.230) | copy-start | bytes 2356 | tf_op jit(solution)/shard_map/while
  16.7 128.7 %all-reduce.24.cloned.1.call-start = ((), (), s32[]{:S(2)}) async-start(), calls=%async_computation.15 | async-start | bytes 2408448 | tf_op jit(solution)/shard_map/while
  89.1 91.4 %all-gather.13.cloned.1.call-start = ((), (), s32[]{:S(2)}) async-start(), calls=%async_computation.16 | async-start | bytes 1505280 | tf_op jit(solution)/shard_map/while/body/eval_jaxpr/all_gather | solution.py:126
  150.2 148.2 %all-reduce.26.cloned.1.call-start = ((), (), s32[]{:S(2)}) async-start(), calls=%async_computation.17 | async-start | bytes 2408448 | tf_op jit(solution)/shard_map/while
  243.0 93.6 %all-gather.7.cloned.1.call-start = ((), (), s32[]{:S(2)}) async-start(), calls=%async_computation.12 | async-start | bytes 1769472 | tf_op jit(solution)/shard_map/while/body/eval_jaxpr/all_gather | solution.py:121
  243.6 110.7 %all-gather.15.cloned.1.call-start = ((), (), s32[]{:S(2)}) async-start(), calls=%async_computation.18 | async-start | bytes 1505280 | tf_op jit(solution)/shard_map/while/body/eval_jaxpr/all_gather | solution.py:126
  301.3 76.5 %all-gather.17.cloned.1.call-start = ((), (), s32[]{:S(2)}) async-start(), calls=%async_computation.19 | async-start | bytes 1769472 | tf_op jit(solution)/shard_map/while/body/eval_jaxpr/all_gather | solution.py:122
  303.1 11.9 collective-permute-start
  304.6 21.4 %collective-permute-start.1 = (bf16[4,49,768]{2,0,1:T(4,128)(2,1)S(1)}, bf16[4,49,768]{2,0,1:T(4,128)(2,1)}, u32[]{:S(2)}, u32[]{:S(2)}) collective-permute-start(bf16[4,49,768]{2,0,1:T(4,128)(2,1)S(1)} %get-tuple-element.862), channel_id=1, source_target_pairs={{0,3},{1,0},{2,1},{3,2},{4,7},{5,4},{6,5},{7,6},{8,11},{9,8},{10,9... | collective-permute-start | bytes 903176 | tf_op jit(solution)/shard_map/while/body/eval_jaxpr/ppermute | solution.py:24
  315.1 16.2 collective-permute-start.2
  315.1 128.1 %all-reduce.28.cloned.1.call-start = ((), (), s32[]{:S(2)}) async-start(), calls=%async_computation.20 | async-start | bytes 2408448 | tf_op jit(solution)/shard_map/while
  451.3 12.1 collective-permute-start.3
  452.7 21.9 %collective-permute-start.4 = (bf16[4,49,768]{2,0,1:T(4,128)(2,1)}, bf16[4,49,768]{2,0,1:T(4,128)(2,1)}, u32[]{:S(2)}, u32[]{:S(2)}) collective-permute-start(bf16[4,49,768]{2,0,1:T(4,128)(2,1)} %get-tuple-element.867), channel_id=1, source_target_pairs={{0,3},{1,0},{2,1},{3,2},{4,7},{5,4},{6,5},{7,6},{8,11},{9,8},{10,9... | collective-permute-start | bytes 903176 | tf_op jit(solution)/shard_map/while/body/eval_jaxpr/ppermute | solution.py:24
  463.4 16.5 collective-permute-start.5
  526.9 22.4 %all-to-all-start.3 = ((bf16[3,16,49,192]{3,2,0,1:T(8,128)(2,1)}), bf16[3,16,49,192]{3,2,0,1:T(8,128)(2,1)}, u32[]{:S(2)}, u32[]{:S(2)}) async-start(bf16[3,16,49,192]{3,2,0,1:T(8,128)(2,1)} %copy.371), calls=%async_computation.3 | async-start | bytes 2752512 | tf_op jit(solution)/shard_map/while/body/eval_jaxpr/all_to_all | solution.py:179
  531.3 80.3 %all-reduce.30.cloned.1.call-start = ((), (), s32[]{:S(2)}) async-start(), calls=%async_computation.21 | async-start | bytes 2408448 | tf_op jit(solution)/shard_map/while
  554.0 207.0 %all-reduce.32.cloned.1.call-start = ((), (), s32[]{:S(2)}) async-start(), calls=%async_computation.22 | async-start | bytes 4816896 | tf_op jit(solution)/shard_map/while
  621.4 12.2 collective-permute-start.6
  626.1 17.4 %collective-permute-start.7 = (bf16[4,49,768]{2,0,1:T(4,128)(2,1)}, bf16[4,49,768]{2,0,1:T(4,128)(2,1)}, u32[]{:S(2)}, u32[]{:S(2)}) collective-permute-start(bf16[4,49,768]{2,0,1:T(4,128)(2,1)} %get-tuple-element.873), channel_id=1, source_target_pairs={{0,3},{1,0},{2,1},{3,2},{4,7},{5,4},{6,5},{7,6},{8,11},{9,8},{10,9... | collective-permute-start | bytes 903176 | tf_op jit(solution)/shard_map/while/body/eval_jaxpr/ppermute | solution.py:24
  633.6 14.3 collective-permute-start.8
  670.0 91.0 %copy-start.4 = (bf16[2,4,49,768]{3,1,2,0:T(4,128)(2,1)S(1)}, bf16[2,4,49,768]{3,1,2,0:T(4,128)(2,1)}, u32[]{:S(2)}) copy-start(bf16[2,4,49,768]{3,1,2,0:T(4,128)(2,1)} %get-tuple-element.990) | copy-start | bytes 1806340 | tf_op jit(solution)/shard_map/while
  670.0 91.0 %copy-start.59 = (f32[768]{0:T(1024)S(1)}, f32[768]{0:T(1024)}, u32[]{:S(2)}) copy-start(f32[768]{0:T(1024)} %copy-done.58) | copy-start | bytes 9220 | tf_op jit(solution)/shard_map/while
  670.0 92.4 %copy-start.51 = (f32[4,49]{0,1:T(8,128)S(1)}, f32[4,49]{0,1:T(8,128)}, u32[]{:S(2)}) copy-start(f32[4,49]{0,1:T(8,128)} %copy-done.50) | copy-start | bytes 2356 | tf_op jit(solution)/shard_map/while
  670.0 92.4 %copy-start.40 = (f32[4,49]{0,1:T(8,128)S(1)}, f32[4,49]{0,1:T(8,128)}, u32[]{:S(2)}) copy-start(f32[4,49]{0,1:T(8,128)} %copy-done.39) | copy-start | bytes 2356 | tf_op jit(solution)/shard_map/while
  670.0 94.3 %copy-start.93 = (f32[768]{0:T(1024)S(1)}, f32[768]{0:T(1024)}, u32[]{:S(2)}) copy-start(f32[768]{0:T(1024)} %get-tuple-element.1001) | copy-start | bytes 9220 | tf_op jit(solution)/shard_map/while
  672.3 92.0 %copy-start.23 = (f32[4,49,768]{2,0,1:T(4,128)S(1)}, f32[4,49,768]{2,0,1:T(4,128)}, u32[]{:S(2)}) copy-start(f32[4,49,768]{2,0,1:T(4,128)} %get-tuple-element.893) | copy-start | bytes 1806340 | tf_op jit(solution)/shard_map/while
  767.7 35.7 %all-gather.11.cloned.1.call-start = ((), (), s32[]{:S(2)}) async-start(), calls=%async_computation.14 | async-start | bytes 2654208 | tf_op jit(solution)/shard_map/while/body/eval_jaxpr/all_gather | solution.py:119
  768.3 67.0 %all-gather.9.cloned.1.call-start = ((), (), s32[]{:S(2)}) async-start(), calls=%async_computation.13 | async-start | bytes 1505280 | tf_op jit(solution)/shard_map/while/body/eval_jaxpr/all_gather | solution.py:126
  770.9 67.0 %copy-start.58 = (f32[768]{0:T(1024)}, f32[768]{0:T(1024)S(1)}, u32[]{:S(2)}) copy-start(f32[768]{0:T(1024)S(1)} %get-tuple-element.842) | copy-start | bytes 9220 | tf_op jit(solution)/shard_map/while
  770.9 131.4 %copy-start.56 = (f32[768]{0:T(1024)}, f32[768]{0:T(1024)S(1)}, u32[]{:S(2)}) copy-start(f32[768]{0:T(1024)S(1)} %get-tuple-element.834) | copy-start | bytes 9220 | tf_op jit(solution)/shard_map/while
  774.8 124.9 %all-reduce.24.cloned.1.call-start = ((), (), s32[]{:S(2)}) async-start(), calls=%async_computation.15 | async-start | bytes 2408448 | tf_op jit(solution)/shard_map/while
  843.4 91.3 %all-gather.13.cloned.1.call-start = ((), (), s32[]{:S(2)}) async-start(), calls=%async_computation.16 | async-start | bytes 1505280 | tf_op jit(solution)/shard_map/while/body/eval_jaxpr/all_gather | solution.py:126
  904.4 148.0 %all-reduce.26.cloned.1.call-start = ((), (), s32[]{:S(2)}) async-start(), calls=%async_computation.17 | async-start | bytes 2408448 | tf_op jit(solution)/shard_map/while
  997.1 93.4 %all-gather.7.cloned.1.call-start = ((), (), s32[]{:S(2)}) async-start(), calls=%async_computation.12 | async-start | bytes 1769472 | tf_op jit(solution)/shard_map/while/body/eval_jaxpr/all_gather | solution.py:121
  997.7 110.5 %all-gather.15.cloned.1.call-start = ((), (), s32[]{:S(2)}) async-start(), calls=%async_computation.18 | async-start | bytes 1505280 | tf_op jit(solution)/shard_map/while/body/eval_jaxpr/all_gather | solution.py:126
  1055.5 76.3 %all-gather.17.cloned.1.call-start = ((), (), s32[]{:S(2)}) async-start(), calls=%async_computation.19 | async-start | bytes 1769472 | tf_op jit(solution)/shard_map/while/body/eval_jaxpr/all_gather | solution.py:122
  1057.3 11.9 collective-permute-start
  1058.7 21.2 %collective-permute-start.1 = (bf16[4,49,768]{2,0,1:T(4,128)(2,1)S(1)}, bf16[4,49,768]{2,0,1:T(4,128)(2,1)}, u32[]{:S(2)}, u32[]{:S(2)}) collective-permute-start(bf16[4,49,768]{2,0,1:T(4,128)(2,1)S(1)} %get-tuple-element.862), channel_id=1, source_target_pairs={{0,3},{1,0},{2,1},{3,2},{4,7},{5,4},{6,5},{7,6},{8,11},{9,8},{10,9... | collective-permute-start | bytes 903176 | tf_op jit(solution)/shard_map/while/body/eval_jaxpr/ppermute | solution.py:24
  1069.2 16.0 collective-permute-start.2
  1069.2 128.0 %all-reduce.28.cloned.1.call-start = ((), (), s32[]{:S(2)}) async-start(), calls=%async_computation.20 | async-start | bytes 2408448 | tf_op jit(solution)/shard_map/while
  1205.3 12.1 collective-permute-start.3
  1206.7 21.9 %collective-permute-start.4 = (bf16[4,49,768]{2,0,1:T(4,128)(2,1)}, bf16[4,49,768]{2,0,1:T(4,128)(2,1)}, u32[]{:S(2)}, u32[]{:S(2)}) collective-permute-start(bf16[4,49,768]{2,0,1:T(4,128)(2,1)} %get-tuple-element.867), channel_id=1, source_target_pairs={{0,3},{1,0},{2,1},{3,2},{4,7},{5,4},{6,5},{7,6},{8,11},{9,8},{10,9... | collective-permute-start | bytes 903176 | tf_op jit(solution)/shard_map/while/body/eval_jaxpr/ppermute | solution.py:24
  1217.4 16.5 collective-permute-start.5
  1280.9 22.4 %all-to-all-start.3 = ((bf16[3,16,49,192]{3,2,0,1:T(8,128)(2,1)}), bf16[3,16,49,192]{3,2,0,1:T(8,128)(2,1)}, u32[]{:S(2)}, u32[]{:S(2)}) async-start(bf16[3,16,49,192]{3,2,0,1:T(8,128)(2,1)} %copy.371), calls=%async_computation.3 | async-start | bytes 2752512 | tf_op jit(solution)/shard_map/while/body/eval_jaxpr/all_to_all | solution.py:179
  1285.3 80.3 %all-reduce.30.cloned.1.call-start = ((), (), s32[]{:S(2)}) async-start(), calls=%async_computation.21 | async-start | bytes 2408448 | tf_op jit(solution)/shard_map/while
  1308.0 207.0 %all-reduce.32.cloned.1.call-start = ((), (), s32[]{:S(2)}) async-start(), calls=%async_computation.22 | async-start | bytes 4816896 | tf_op jit(solution)/shard_map/while
  1375.4 12.2 collective-permute-start.6
  1380.1 17.4 %collective-permute-start.7 = (bf16[4,49,768]{2,0,1:T(4,128)(2,1)}, bf16[4,49,768]{2,0,1:T(4,128)(2,1)}, u32[]{:S(2)}, u32[]{:S(2)}) collective-permute-start(bf16[4,49,768]{2,0,1:T(4,128)(2,1)} %get-tuple-element.873), channel_id=1, source_target_pairs={{0,3},{1,0},{2,1},{3,2},{4,7},{5,4},{6,5},{7,6},{8,11},{9,8},{10,9... | collective-permute-start | bytes 903176 | tf_op jit(solution)/shard_map/while/body/eval_jaxpr/ppermute | solution.py:24
  1387.6 14.3 collective-permute-start.8
  1424.0 91.0 %copy-start.4 = (bf16[2,4,49,768]{3,1,2,0:T(4,128)(2,1)S(1)}, bf16[2,4,49,768]{3,1,2,0:T(4,128)(2,1)}, u32[]{:S(2)}) copy-start(bf16[2,4,49,768]{3,1,2,0:T(4,128)(2,1)} %get-tuple-element.990) | copy-start | bytes 1806340 | tf_op jit(solution)/shard_map/while
  1424.0 91.0 %copy-start.59 = (f32[768]{0:T(1024)S(1)}, f32[768]{0:T(1024)}, u32[]{:S(2)}) copy-start(f32[768]{0:T(1024)} %copy-done.58) | copy-start | bytes 9220 | tf_op jit(solution)/shard_map/while
  1424.0 92.4 %copy-start.51 = (f32[4,49]{0,1:T(8,128)S(1)}, f32[4,49]{0,1:T(8,128)}, u32[]{:S(2)}) copy-start(f32[4,49]{0,1:T(8,128)} %copy-done.50) | copy-start | bytes 2356 | tf_op jit(solution)/shard_map/while
  1424.0 92.4 %copy-start.40 = (f32[4,49]{0,1:T(8,128)S(1)}, f32[4,49]{0,1:T(8,128)}, u32[]{:S(2)}) copy-start(f32[4,49]{0,1:T(8,128)} %copy-done.39) | copy-start | bytes 2356 | tf_op jit(solution)/shard_map/while
  1424.0 94.3 %copy-start.93 = (f32[768]{0:T(1024)S(1)}, f32[768]{0:T(1024)}, u32[]{:S(2)}) copy-start(f32[768]{0:T(1024)} %get-tuple-element.1001) | copy-start | bytes 9220 | tf_op jit(solution)/shard_map/while
  1428.4 89.9 %copy-start.23 = (f32[4,49,768]{2,0,1:T(4,128)S(1)}, f32[4,49,768]{2,0,1:T(4,128)}, u32[]{:S(2)}) copy-start(f32[4,49,768]{2,0,1:T(4,128)} %get-tuple-element.893) | copy-start | bytes 1806340 | tf_op jit(solution)/shard_map/while
  1525.4 56.9 %reduce-scatter.13.cloned.1.call-start = ((), (), s32[]{:S(2)}) async-start(), calls=%async_computation.11 | async-start | bytes 1327104
  1530.2 81.9 %reduce-scatter.11.cloned.1.call-start = ((), (), s32[]{:S(2)}) async-start(), calls=%async_computation.10 | async-start | bytes 2654208 | tf_op jit(solution)/shard_map/reduce_scatter | solution.py:306
  1533.5 124.7 %reduce-scatter.9.cloned.1.call-start = ((), (), s32[]{:S(2)}) async-start(), calls=%async_computation.9 | async-start | bytes 2654208 | tf_op jit(solution)/shard_map/reduce_scatter | solution.py:305
  1534.0 181.7 %reduce-scatter.7.cloned.1.call-start = ((), (), s32[]{:S(2)}) async-start(), calls=%async_computation.8 | async-start | bytes 5308416 | tf_op jit(solution)/shard_map/reduce_scatter | solution.py:303
  (184 other events, 1584.1 us)
Sparse Core Ops, SparseCore 0:
  11.8 34.7 all-gather.10
  48.8 32.1 all-gather.8
  89.3 56.1 all-reduce.23
  150.3 30.1 all-gather.12
  243.1 55.1 all-reduce.25
  299.7 22.2 all-gather.6
  323.6 30.6 all-gather.14
  355.8 21.9 all-gather.16
  386.3 56.8 all-reduce.27
  554.1 57.3 all-reduce.29
  662.9 98.0 all-reduce.31
  769.7 33.5 all-gather.10
  805.5 29.7 all-gather.8
  843.5 56.1 all-reduce.23
  904.6 30.1 all-gather.12
  997.2 55.1 all-reduce.25
  1053.9 22.2 all-gather.6
  1077.5 30.6 all-gather.14
  1109.8 21.9 all-gather.16
  1140.3 56.8 all-reduce.27
  1308.1 57.3 all-reduce.29
  1416.9 98.0 all-reduce.31
Sparse Core Ops, SparseCore 1:
  1530.3 35.7 reduce-scatter.12
  1569.9 42.2 reduce-scatter.10
  1615.9 42.2 reduce-scatter.8
  1662.2 53.5 reduce-scatter.6
